TPU v7x, 32 devices: a whole 2x2x4 slice. The times are simulated.
32 devices in a mesh: lon: 8 (over z, x), lat: 4 (over y, core).
Axes of the slice: x: 2, y: 2, z: 4, core: 2. Of those that a mesh axis runs over, the one named last changes fastest.
Arguments:
- fields: bfloat16 [128, 256, 256], P('lat', 'lon'), may hold values from -6 to 6
- cotangent: bfloat16 [128, 256, 256], P('lat', 'lon'), may hold values from -6 to 6
- dw_kernel: bfloat16 [7, 7, 256], replicated, may hold values from -0.875 to 0.875
- dw_bias: bfloat16 [256], replicated, may hold values from -3 to 3
- norm_gain: bfloat16 [256], replicated, may hold values from 0.099609375 to 1.8984375
- layer_norm_offset: bfloat16 [256], replicated, may hold values from -3 to 3
- w_expand: bfloat16 [256, 1024], replicated, may hold values from -0.375 to 0.375
- b_expand: bfloat16 [1024], replicated, may hold values from -3 to 3
- w_project: bfloat16 [1024, 256], replicated, may hold values from -0.1875 to 0.1875
- b_project: bfloat16 [256], replicated, may hold values from -3 to 3
Outputs:
- block_out: bfloat16 [128, 256, 256], P('lat', 'lon')
- grad_fields: bfloat16 [128, 256, 256], P('lat', 'lon')
- grad_kernel: float32 [7, 7, 256], replicated
- grad_dw_bias: float32 [256], replicated
- grad_gain: float32 [256], replicated
- grad_shift: float32 [256], replicated
- grad_expand: float32 [256, 1024], replicated
- grad_b_expand: float32 [1024], replicated
- grad_project: float32 [1024, 256], replicated
- grad_b_project: float32 [256], replicated
All inputs are finite; a program needn't handle non-finite values.
Results may differ from a plain program's by a relative error of at most 0.0075.
Values may be sent and summed in bfloat16 or wider, within the bound.
No kernel may reach another device: no remote copies, remote signals or barrier semaphores. Data moves between devices by JAX's collectives and lax.ppermute only.
A program may use at most 64 MiB of HBM per device.

v0:
```python
import math
import jax
import jax.numpy as jnp
from jax import lax
from jax.sharding import PartitionSpec as P

EPS = 1e-06


def extended(array, sides, width, wrap):
    for axis, dim in sides:
        size, length = (lax.axis_size(axis), array.shape[dim])
        up = [(i, (i + 1) % size) for i in range(size if wrap else size - 1)]
        down = [(j, i) for i, j in up]
        last = lax.slice_in_dim(array, length - width, length, axis=dim)
        first = lax.slice_in_dim(array, 0, width, axis=dim)
        before = lax.ppermute(last, axis, up)
        after = lax.ppermute(first, axis, down)
        array = jnp.concatenate([before, array, after], axis=dim)
    return array


def from_behind(value, axis, steps):
    count = lax.axis_size(axis)
    pairs = [(source, (source + steps) % count) for source in range(count)]
    return lax.ppermute(value, axis, pairs)


def gelu_parts(values):
    normal_cdf = 0.5 * (1.0 + jax.scipy.special.erf(values * (1.0 / math.sqrt(2.0))))
    density = jnp.exp(-0.5 * values * values) * (1.0 / math.sqrt(2.0 * math.pi))
    return (values * normal_cdf, normal_cdf + values * density)


def contract_rows(left, right):
    return lax.dot_general(
        left, right, (((0,), (0,)), ((), ())), preferred_element_type=jnp.float32
    )


def sphere_pad(field):
    lat_index = lax.axis_index("lat")
    north = lat_index == 0
    south = lat_index == lax.axis_size("lat") - 1
    wide = extended(field, (("lon", 1),), 3, True)
    outgoing = jnp.where(north, wide[2::-1], wide[:-4:-1])
    partner = from_behind(outgoing, "lon", lax.axis_size("lon") // 2)
    tall = extended(wide, (("lat", 0),), 3, False)
    top_rows = jnp.where(north, partner, tall[:3])
    bottom_rows = jnp.where(south, partner, tall[-3:])
    return (jnp.concatenate([top_rows, tall[3:-3], bottom_rows], axis=0), north, south)


def local(
    fields,
    cotangent,
    dw_kernel,
    dw_bias,
    norm_gain,
    layer_norm_offset,
    w_expand,
    b_expand,
    w_project,
    b_project,
):
    rows = fields.shape[0]
    cols = fields.shape[1]
    chans = fields.shape[2]
    scale_factor = 1.0 / math.sqrt(rows * cols * lax.axis_size("lat") * lax.axis_size("lon"))
    weights = dw_kernel.astype(jnp.float32)
    norm_scale_factor = norm_gain.astype(jnp.float32)
    padded, north, south = sphere_pad(fields)
    conv = jnp.zeros((rows, cols, chans), jnp.float32)
    for row_off in range(7):
        for col_off in range(7):
            conv = conv + weights[row_off, col_off] * padded[
                row_off : row_off + rows, col_off : col_off + cols
            ].astype(jnp.float32)
    conv = conv.reshape(-1, chans) + dw_bias.astype(jnp.float32)
    mean_removed = conv - jnp.mean(conv, axis=-1, keepdims=True)
    inverse_deviation = lax.rsqrt(
        jnp.mean(mean_removed * mean_removed, axis=-1, keepdims=True) + EPS
    )
    standardized_input = mean_removed * inverse_deviation
    normalized_input = (
        standardized_input * norm_scale_factor + layer_norm_offset.astype(jnp.float32)
    ).astype(jnp.bfloat16)
    pre = jnp.dot(normalized_input, w_expand, preferred_element_type=jnp.float32) + b_expand.astype(
        jnp.float32
    )
    active, slope = gelu_parts(pre)
    hidden = active.astype(jnp.bfloat16)
    branch = jnp.dot(hidden, w_project, preferred_element_type=jnp.float32) + b_project.astype(
        jnp.float32
    )
    flat_fields = fields.reshape(-1, chans)
    block_out = (
        (flat_fields.astype(jnp.float32) + branch).astype(jnp.bfloat16).reshape(rows, cols, chans)
    )
    flat_cot = cotangent.reshape(-1, chans)
    grad_proj = contract_rows(hidden, flat_cot) * scale_factor
    grad_bproj = jnp.sum(flat_cot.astype(jnp.float32), axis=0) * scale_factor
    d_hidden = jnp.dot(flat_cot, w_project.T, preferred_element_type=jnp.float32)
    d_pre = (d_hidden * slope).astype(jnp.bfloat16)
    grad_exp = contract_rows(normalized_input, d_pre) * scale_factor
    grad_bexp = jnp.sum(d_pre.astype(jnp.float32), axis=0) * scale_factor
    normalized_gradient = jnp.dot(d_pre, w_expand.T, preferred_element_type=jnp.float32)
    gain_gradient = jnp.sum(normalized_gradient * standardized_input, axis=0) * scale_factor
    grad_sh = jnp.sum(normalized_gradient, axis=0) * scale_factor
    scaled_output = normalized_gradient * norm_scale_factor
    conv_gradient = inverse_deviation * (
        scaled_output
        - jnp.mean(scaled_output, axis=-1, keepdims=True)
        - standardized_input * jnp.mean(scaled_output * standardized_input, axis=-1, keepdims=True)
    )
    conv_gradient = conv_gradient.astype(jnp.bfloat16).reshape(rows, cols, chans)
    grad_dwb = jnp.sum(conv_gradient.astype(jnp.float32), axis=(0, 1)) * scale_factor
    dconv_wide = conv_gradient.astype(jnp.float32)
    kern_terms = []
    for row_off in range(7):
        for col_off in range(7):
            window = padded[row_off : row_off + rows, col_off : col_off + cols].astype(jnp.float32)
            kern_terms.append(jnp.sum(dconv_wide * window, axis=(0, 1)))
    grad_kern = jnp.stack(kern_terms, axis=0).reshape(7, 7, chans) * scale_factor
    dpad, north, south = sphere_pad(conv_gradient)
    zero_rows = jnp.zeros((3, cols + 6, chans), jnp.bfloat16)
    inner = jnp.concatenate(
        [jnp.where(north, zero_rows, dpad[:3]), dpad[3:-3], jnp.where(south, zero_rows, dpad[-3:])],
        axis=0,
    )
    spacer = jnp.zeros((6, cols + 6, chans), jnp.bfloat16)
    fold_north = jnp.concatenate([jnp.where(north, dpad[:3], zero_rows), spacer], axis=0)
    fold_south = jnp.concatenate([spacer, jnp.where(south, dpad[-3:], zero_rows)], axis=0)
    adjoint = jnp.zeros((rows, cols, chans), jnp.float32)
    north_term = jnp.zeros((3, cols, chans), jnp.float32)
    south_term = jnp.zeros((3, cols, chans), jnp.float32)
    for row_off in range(7):
        for col_off in range(7):
            weight = weights[row_off, col_off]
            col_from = 6 - col_off
            adjoint = adjoint + weight * inner[
                6 - row_off : 6 - row_off + rows, col_from : col_from + cols
            ].astype(jnp.float32)
            north_term = north_term + weight * fold_north[
                row_off : row_off + 3, col_from : col_from + cols
            ].astype(jnp.float32)
            south_term = south_term + weight * fold_south[
                row_off : row_off + 3, col_from : col_from + cols
            ].astype(jnp.float32)
    adjoint = adjoint.at[:3].add(north_term)
    adjoint = adjoint.at[rows - 3 :].add(south_term)
    grad_fields = (cotangent.astype(jnp.float32) + adjoint).astype(jnp.bfloat16)
    sum_kern, sum_dwb, sum_gn, sum_sh, sum_exp, sum_bexp, sum_proj, sum_bproj = lax.psum(
        (grad_kern, grad_dwb, gain_gradient, grad_sh, grad_exp, grad_bexp, grad_proj, grad_bproj),
        ("lon", "lat"),
    )
    return (
        block_out,
        grad_fields,
        sum_kern,
        sum_dwb,
        sum_gn,
        sum_sh,
        sum_exp,
        sum_bexp,
        sum_proj,
        sum_bproj,
    )


def solution(mesh):
    placed = (P("lat", "lon", None), P("lat", "lon", None), P(), P(), P(), P(), P(), P(), P(), P())
    return jax.shard_map(
        local,
        mesh=mesh,
        in_specs=placed,
        out_specs=(
            P("lat", "lon", None),
            P("lat", "lon", None),
            P(),
            P(),
            P(),
            P(),
            P(),
            P(),
            P(),
            P(),
        ),
        check_vma=False,
    )
```

profile of v0, /device:TPU:0, one launch (start us, length us, event | category | flops | bytes accessed | tf_op | source)
XLA Modules:
  0.0 221.7 jit_solution(7986544816358134473)
XLA Ops:
  7.2 0.0 copy-start
  7.2 0.0 all-reduce.6.cloned.1.call-start
  7.2 1.1 fusion.150
  8.4 3.0 %collective-permute-start = (bf16[32,3,256]{2,1,0:T(4,128)(2,1)S(1)}, bf16[32,3,256]{2,1,0:T(4,128)(2,1)S(1)}, u32[]{:S(2)}, u32[]{:S(2)}) collective-permute-start(bf16[32,3,256]{2,1,0:T(4,128)(2,1)S(1)} %get-tuple-element.121), channel_id=1, source_target_pairs={{0,4},{4,8},{8,12},{12,16},{16,20},{20,24},{24,28},{28,0},{1,5},{5... | collective-permute-start | bytes 147464 | tf_op jit(solution)/shard_map/ppermute | solution.py:17
  11.4 3.1 %collective-permute-start.1 = (bf16[32,3,256]{2,1,0:T(4,128)(2,1)S(1)}, bf16[32,3,256]{2,1,0:T(4,128)(2,1)S(1)}, u32[]{:S(2)}, u32[]{:S(2)}) collective-permute-start(bf16[32,3,256]{2,1,0:T(4,128)(2,1)S(1)} %get-tuple-element.122), channel_id=1, source_target_pairs={{4,0},{8,4},{12,8},{16,12},{20,16},{24,20},{28,24},{0,28},{5,1},{9... | collective-permute-start | bytes 147464 | tf_op jit(solution)/shard_map/ppermute | solution.py:18
  14.5 1.0 fusion.151
  15.5 1.0 fusion.152
  16.5 1.0 fusion.153
  17.6 0.5 broadcast_multiply_fusion.19
  18.1 0.6 broadcast_multiply_fusion.9
  18.7 0.6 broadcast_multiply_fusion.11
  19.2 0.6 broadcast_multiply_fusion.13
  19.8 0.6 broadcast_multiply_fusion.15
  20.4 0.6 broadcast_multiply_fusion.17
  21.0 0.6 fusion.147
  21.6 1.1 constant_dynamic-update-slice_fusion.1
  22.7 0.7 convert_element_type.576
  23.3 0.7 convert_element_type.577
  24.0 0.7 convert_element_type.580
  24.7 0.7 convert_element_type.578
  25.3 1.2 convert_element_type.582
  26.6 0.9 pad_maximum_fusion.10
  27.4 1.5 collective-permute-start.3
  28.9 1.3 collective-permute-start.4
  30.2 0.8 collective-permute-start.2
  31.1 4.3 %collective-permute-done.2 = bf16[3,38,256]{2,1,0:T(8,128)(2,1)S(1)} collective-permute-done((bf16[3,38,256]{2,1,0:T(8,128)(2,1)S(1)}, bf16[3,38,256]{2,1,0:T(8,128)(2,1)S(1)}, u32[]{:S(2)}, u32[]{:S(2)}) %collective-permute-start.2) | collective-permute-done | bytes 58400 | tf_op jit(solution)/shard_map/ppermute | solution.py:26
  35.5 0.4 maximum_maximum_fusion
  35.9 8.6 %add_reduce_fusion = (f32[32,32]{1,0:T(8,128)S(1)}, f32[32,32,256]{2,1,0:T(8,128)}) fusion(f32[256]{0:T(256)S(1)} %convert_element_type.576, bf16[35,38,256]{2,1,0:T(8,128)(2,1)S(1)} %get-tuple-element.114, f32[256]{0:T(256)S(1)} %bitcast.258, f32[256]{0:T(256)S(1)} %bitcast.254, f32[256]{0:T(256)S(1)} %bitcast.250, f32[256]{0:T(256)S(1)} %bitcast.246, ...), kind=kLoop, calls=%fused_computation.247 | loop fusion | flops 41155584 | bytes 25270272 | tf_op jit(solution)/shard_map/reduce_sum | solution.py:80
  44.5 0.1 div.15
  44.5 1.6 multiply_reduce_fusion.2
  46.2 0.1 rsqrt.12
  46.2 1.6 fusion.132
  47.8 1.2 multiply_convert_fusion
  49.0 2.5 %convert_reduce_fusion = (f32[1024]{0:T(1024)S(1)}, bf16[1024,1024]{1,0:T(8,128)(2,1)S(1)}) fusion(f32[1024,1024]{1,0:T(8,128)S(1)} %get-tuple-element.181, f32[1024]{0:T(1024)S(1)} %convert_element_type.580, bf16[1024,256]{1,0:T(8,128)(2,1)S(1)} %bitcast.175, bf16[1024,256]{1,0:T(8,128)(2,1)S(1)} %copy-done.22), kind=kOutput, calls=%fused_computation.57 | convolution fusion | flops 550501376 | bytes 7348224 | tf_op jit(solution)/shard_map/dot_general | solution.py:103
  51.5 1.7 convolution_multiply_fusion.1
  53.3 1.4 multiply_reduce_fusion
  54.7 0.9 convert_reduce_fusion.2
  55.6 3.2 %fusion.130 = (f32[256]{0:T(256)S(1)}, f32[256]{0:T(256)S(1)}, f32[256]{0:T(256)S(1)}, f32[256]{0:T(256)S(1)}, f32[256]{0:T(256)S(1)}, /*index=5*/f32[256]{0:T(2...) fusion(bf16[35,38,256]{2,1,0:T(8,128)(2,1)S(1)} %get-tuple-elem, ...), kind=kLoop, calls=%fused_computation.237 | loop fusion | flops 14413312 | bytes 9979904 | tf_op jit(solution)/shard_map/reduce_sum | solution.py:123
  58.8 3.2 %fusion.102 = (f32[256]{0:T(256)}, f32[256]{0:T(256)}, f32[256]{0:T(256)}, f32[256]{0:T(256)}, f32[256]{0:T(256)}, /*index=5*/f32[256]{0:T(256)}, f32[256]{0:T(2...) fusion(bf16[35,38,256]{2,1,0:T(8,128)(2,1)S(1)} %get-tuple-elem, ...), kind=kLoop, calls=%fused_computation.209 | loop fusion | flops 14413312 | bytes 9979904 | tf_op jit(solution)/shard_map/reduce_sum | solution.py:123
  62.1 1.7 convolution_multiply_fusion
  63.8 3.5 %fusion.112 = (f32[256]{0:T(256)S(1)}, f32[256]{0:T(256)S(1)}, f32[256]{0:T(256)S(1)}, f32[256]{0:T(256)S(1)}, f32[256]{0:T(256)S(1)}, /*index=5*/f32[256]{0:T(2...) fusion(bf16[35,38,256]{2,1,0:T(8,128)(2,1)S(1)} %get-tuple-elem, ...), kind=kLoop, calls=%fused_computation.219 | loop fusion | flops 12841728 | bytes 5829632 | tf_op jit(solution)/shard_map/reduce_sum | solution.py:123
  67.3 0.0 copy-start.23
  67.4 0.0 copy-start.24
  67.4 4.4 %stack.199 = f32[49,256]{1,0:T(8,128)S(1)} concatenate(f32[1,256]{1,0:T(1,128)S(1)} %bitcast.376, f32[1,256]{1,0:T(1,128)S(1)} %bitcast.377, f32[1,256]{1,0:T(1,128)S(1)} %bitcast.378, f32[1,256]{1,0:T(1,128)} %bitcast.421, f32[1,256]{1,0:T(1,128)} %bitcast.420, f32[1,256]{1,0:T(1,128)} %bitcast.419, f32[1,256]{1,0:T(1,128)} %bitcast.418, f32[1,256]{1,0:T(1,128)} %bitcast.417, ...), dimensions={0} | concatenate | bytes 100352 | tf_op jit(solution)/shard_map/stack | solution.py:124
  71.7 0.1 fusion.149
  71.8 0.1 collective-permute-start.5
  71.9 4.7 %collective-permute-start.6 = (bf16[32,3,256]{2,1,0:T(4,128)(2,1)S(1)}, bf16[32,3,256]{2,1,0:T(4,128)(2,1)S(1)}, u32[]{:S(2)}, u32[]{:S(2)}) collective-permute-start(bf16[32,3,256]{2,1,0:T(4,128)(2,1)S(1)} %get-tuple-element.119), channel_id=1, source_target_pairs={{4,0},{8,4},{12,8},{16,12},{20,16},{24,20},{28,24},{0,28},{5,1},{9... | collective-permute-start | bytes 147464 | tf_op jit(solution)/shard_map/ppermute | solution.py:18
  76.6 0.0 all-reduce.6.cloned.1.call-update
  76.7 3.1 %fusion.7 = bf16[1024,256]{1,0:T(8,128)(2,1)} fusion(bf16[1024,1024]{1,0:T(8,128)(2,1)} %copy-done.4, bf16[1024,256]{1,0:T(8,128)(2,1)S(1)} %copy-done.23, f32[256]{0:T(256)S(1)} %copy-done.24, bf16[1024,256]{1,0:T(8,128)(2,1)S(1)} %bitcast.174), kind=kOutput, calls=%fused_computation.114 | convolution fusion | flops 537919488 | bytes 3671040 | tf_op jit(solution)/shard_map/dot_general | solution.py:93
  79.8 1.3 collective-permute-start.8
  81.2 3.7 %collective-permute-start.9 = (bf16[3,38,256]{2,1,0:T(8,128)(2,1)S(1)}, bf16[3,38,256]{2,1,0:T(8,128)(2,1)S(1)}, u32[]{:S(2)}, u32[]{:S(2)}) collective-permute-start(bf16[3,38,256]{2,1,0:T(8,128)(2,1)S(1)} %get-tuple-element.112), channel_id=1, source_target_pairs={{0,1},{1,2},{2,3},{4,5},{5,6},{6,7},{8,9},{9,10},{10,11},{12,13},{... | collective-permute-start | bytes 175112 | tf_op jit(solution)/shard_map/ppermute | solution.py:17
  84.8 0.1 collective-permute-start.7
  85.0 6.9 %collective-permute-done.7 = bf16[3,38,256]{2,1,0:T(8,128)(2,1)S(1)} collective-permute-done((bf16[3,38,256]{2,1,0:T(8,128)(2,1)S(1)}, bf16[3,38,256]{2,1,0:T(8,128)(2,1)S(1)}, u32[]{:S(2)}, u32[]{:S(2)}) %collective-permute-start.7) | collective-permute-done | bytes 58400 | tf_op jit(solution)/shard_map/ppermute | solution.py:26
  91.9 0.4 pad_maximum_fusion.1
  92.3 0.0 copy-start.9
  92.4 0.0 copy-start.10
  92.5 8.0 %fusion.81 = f32[32,32,256]{2,1,0:T(8,128)S(1)} fusion(bf16[32,32,256]{2,1,0:T(8,128)(2,1)S(1)} %bitcast.173, bf16[32,3,256]{2,1,0:T(4,128)(2,1)S(1)} %collective-permute-done.5, bf16[32,3,256]{2,1,0:T(4,128)(2,1)S(1)} %collective-permute-done.6, bf16[35,38,256]{2,1,0:T(8,128)(2,1)S(1)} %get-tuple-element.110, ...), kind=kLoop, calls=%fused_computation.188 | loop fusion | flops 42991616 | bytes 23741440 | tf_op jit(solution)/shard_map/add | solution.py:141
  100.6 0.4 fusion.141
  101.1 0.2 fusion.140
  101.3 1.1 convert_reduce_fusion.1
  102.3 41.5 %all-reduce.2 = (f32[7,7,256]{2,1,0:T(8,128)}, f32[256]{0:T(256)}, f32[256]{0:T(256)}, f32[256]{0:T(256)}, f32[1024]{0:T(1024)}, /*index=5*/f32[256]{0:T(256)}) all-reduce(f32[7,7,256]{2,1,0:T(8,128)S(1)} %mul.2248, f32[256]{0:T(256)S(1)} %broadcast_multiply_fusion.8, ...), channel_id=1, replica_groups=mesh['lon'=8,'lat'=4] {'lon','lat'}, use_global_device_ids=true, to_apply=%region_53.54 | all-reduce | flops 14592 | bytes 116736 | tf_op jit(solution)/shard_map/psum | solution.py:153
  143.8 67.6 %all-reduce.6.cloned.1.call-done = (f32[256,1024]{1,0:T(8,128)}, f32[1024,256]{1,0:T(8,128)}) async-done(((f32[256,1024]{1,0:T(8,128)}, f32[1024,256]{1,0:T(8,128)}), (f32[256,1024]{1,0:T(8,128)}, f32[1024,256]{1,0:T(8,128)})) %all-reduce.6.cloned.1.call-update) | async-done | bytes 2097168 | tf_op jit(solution)/shard_map/psum | solution.py:153
  211.5 2.4 %copy.25 = f32[256,1024]{1,0:T(8,128)} copy(f32[256,1024]{1,0:T(8,128)} %get-tuple-element.223) | data formatting | bytes 2097152
  213.9 1.0 copy.26
  (76 shorter events, 0.4 us)
Async XLA Ops:
  7.2 40.6 %copy-start = (bf16[256,1024]{1,0:T(8,128)(2,1)S(1)}, bf16[256,1024]{1,0:T(8,128)(2,1)}, u32[]{:S(2)}) copy-start(bf16[256,1024]{1,0:T(8,128)(2,1)} %param.20) | copy-start | bytes 1572868
  7.2 28.3 %copy-start.2 = (bf16[32,32,256]{2,1,0:T(8,128)(2,1)S(1)}, bf16[32,32,256]{2,1,0:T(8,128)(2,1)}, u32[]{:S(2)}) copy-start(bf16[32,32,256]{2,1,0:T(8,128)(2,1)} %param.14) | copy-start | bytes 1572868
  7.2 204.3 %all-reduce.6.cloned.1.call-start = ((), (), s32[]{:S(2)}) async-start(), calls=%async_computation | async-start | bytes 4194304 | tf_op jit(solution)/shard_map/psum | solution.py:153
  8.4 18.2 %collective-permute-start = (bf16[32,3,256]{2,1,0:T(4,128)(2,1)S(1)}, bf16[32,3,256]{2,1,0:T(4,128)(2,1)S(1)}, u32[]{:S(2)}, u32[]{:S(2)}) collective-permute-start(bf16[32,3,256]{2,1,0:T(4,128)(2,1)S(1)} %get-tuple-element.121), channel_id=1, source_target_pairs={{0,4},{4,8},{8,12},{12,16},{16,20},{20,24},{24,28},{28,0},{1,5},{5... | collective-permute-start | bytes 147464 | tf_op jit(solution)/shard_map/ppermute | solution.py:17
  11.4 15.2 %collective-permute-start.1 = (bf16[32,3,256]{2,1,0:T(4,128)(2,1)S(1)}, bf16[32,3,256]{2,1,0:T(4,128)(2,1)S(1)}, u32[]{:S(2)}, u32[]{:S(2)}) collective-permute-start(bf16[32,3,256]{2,1,0:T(4,128)(2,1)S(1)} %get-tuple-element.122), channel_id=1, source_target_pairs={{4,0},{8,4},{12,8},{16,12},{20,16},{24,20},{28,24},{0,28},{5,1},{9... | collective-permute-start | bytes 147464 | tf_op jit(solution)/shard_map/ppermute | solution.py:18
  27.4 8.0 %collective-permute-start.3 = (bf16[3,38,256]{2,1,0:T(8,128)(2,1)S(1)}, bf16[3,38,256]{2,1,0:T(8,128)(2,1)S(1)}, u32[]{:S(2)}, u32[]{:S(2)}) collective-permute-start(bf16[3,38,256]{2,1,0:T(8,128)(2,1)S(1)} %get-tuple-element.116), channel_id=1, source_target_pairs={{0,1},{1,2},{2,3},{4,5},{5,6},{6,7},{8,9},{9,10},{10,11},{12,13},{... | collective-permute-start | bytes 175112 | tf_op jit(solution)/shard_map/ppermute | solution.py:17
  28.9 6.5 %collective-permute-start.4 = (bf16[3,38,256]{2,1,0:T(8,128)(2,1)S(1)}, bf16[3,38,256]{2,1,0:T(8,128)(2,1)S(1)}, u32[]{:S(2)}, u32[]{:S(2)}) collective-permute-start(bf16[3,38,256]{2,1,0:T(8,128)(2,1)S(1)} %get-tuple-element.115), channel_id=1, source_target_pairs={{1,0},{2,1},{3,2},{5,4},{6,5},{7,6},{9,8},{10,9},{11,10},{13,12},{... | collective-permute-start | bytes 175112 | tf_op jit(solution)/shard_map/ppermute | solution.py:18
  30.2 5.2 %collective-permute-start.2 = (bf16[3,38,256]{2,1,0:T(8,128)(2,1)S(1)}, bf16[3,38,256]{2,1,0:T(8,128)(2,1)S(1)}, u32[]{:S(2)}, u32[]{:S(2)}) collective-permute-start(bf16[3,38,256]{2,1,0:T(8,128)(2,1)S(1)} %reverse_select_fusion.1), channel_id=1, source_target_pairs={{0,16},{4,20},{8,24},{12,28},{16,0},{20,4},{24,8},{28,12},{1,17},{... | collective-permute-start | bytes 175112 | tf_op jit(solution)/shard_map/ppermute | solution.py:26
  47.8 1.2 copy-start.6
  47.8 1.2 copy-start.22
  49.0 13.1 %copy-start.4 = (bf16[1024,1024]{1,0:T(8,128)(2,1)}, bf16[1024,1024]{1,0:T(8,128)(2,1)S(1)}, u32[]{:S(2)}) copy-start(bf16[1024,1024]{1,0:T(8,128)(2,1)S(1)} %get-tuple-element.180) | copy-start | bytes 6291460
  53.3 1.4 copy-start.1
  67.3 9.3 %copy-start.3 = (bf16[32,32,256]{2,1,0:T(8,128)(2,1)S(1)}, bf16[32,32,256]{2,1,0:T(8,128)(2,1)}, u32[]{:S(2)}) copy-start(bf16[32,32,256]{2,1,0:T(8,128)(2,1)} %param.14) | copy-start | bytes 1572868
  67.3 9.3 %copy-start.23 = (bf16[1024,256]{1,0:T(8,128)(2,1)S(1)}, bf16[1024,256]{1,0:T(8,128)(2,1)}, u32[]{:S(2)}) copy-start(bf16[1024,256]{1,0:T(8,128)(2,1)} %param.22) | copy-start | bytes 1572868
  67.4 9.3 %copy-start.24 = (f32[256]{0:T(256)S(1)}, f32[256]{0:T(256)}, u32[]{:S(2)}) copy-start(f32[256]{0:T(256)} %convert_element_type.582) | copy-start | bytes 3076
  71.8 8.0 %collective-permute-start.5 = (bf16[32,3,256]{2,1,0:T(4,128)(2,1)S(1)}, bf16[32,3,256]{2,1,0:T(4,128)(2,1)S(1)}, u32[]{:S(2)}, u32[]{:S(2)}) collective-permute-start(bf16[32,3,256]{2,1,0:T(4,128)(2,1)S(1)} %get-tuple-element.120), channel_id=1, source_target_pairs={{0,4},{4,8},{8,12},{12,16},{16,20},{20,24},{24,28},{28,0},{1,5},{5... | collective-permute-start | bytes 147464 | tf_op jit(solution)/shard_map/ppermute | solution.py:17
  71.9 7.9 %collective-permute-start.6 = (bf16[32,3,256]{2,1,0:T(4,128)(2,1)S(1)}, bf16[32,3,256]{2,1,0:T(4,128)(2,1)S(1)}, u32[]{:S(2)}, u32[]{:S(2)}) collective-permute-start(bf16[32,3,256]{2,1,0:T(4,128)(2,1)S(1)} %get-tuple-element.119), channel_id=1, source_target_pairs={{4,0},{8,4},{12,8},{16,12},{20,16},{24,20},{28,24},{0,28},{5,1},{9... | collective-permute-start | bytes 147464 | tf_op jit(solution)/shard_map/ppermute | solution.py:18
  76.6 3.1 %copy-start.20 = (f32[256]{0:T(256)S(1)}, f32[256]{0:T(256)}, u32[]{:S(2)}) copy-start(f32[256]{0:T(256)} %get-tuple-element.34) | copy-start | bytes 3076
  76.6 3.1 %copy-start.21 = (f32[256]{0:T(256)S(1)}, f32[256]{0:T(256)}, u32[]{:S(2)}) copy-start(f32[256]{0:T(256)} %get-tuple-element.85) | copy-start | bytes 3076
  79.8 12.1 %collective-permute-start.8 = (bf16[3,38,256]{2,1,0:T(8,128)(2,1)S(1)}, bf16[3,38,256]{2,1,0:T(8,128)(2,1)S(1)}, u32[]{:S(2)}, u32[]{:S(2)}) collective-permute-start(bf16[3,38,256]{2,1,0:T(8,128)(2,1)S(1)} %get-tuple-element.111), channel_id=1, source_target_pairs={{1,0},{2,1},{3,2},{5,4},{6,5},{7,6},{9,8},{10,9},{11,10},{13,12},{... | collective-permute-start | bytes 175112 | tf_op jit(solution)/shard_map/ppermute | solution.py:18
  81.2 10.7 %collective-permute-start.9 = (bf16[3,38,256]{2,1,0:T(8,128)(2,1)S(1)}, bf16[3,38,256]{2,1,0:T(8,128)(2,1)S(1)}, u32[]{:S(2)}, u32[]{:S(2)}) collective-permute-start(bf16[3,38,256]{2,1,0:T(8,128)(2,1)S(1)} %get-tuple-element.112), channel_id=1, source_target_pairs={{0,1},{1,2},{2,3},{4,5},{5,6},{6,7},{8,9},{9,10},{10,11},{12,13},{... | collective-permute-start | bytes 175112 | tf_op jit(solution)/shard_map/ppermute | solution.py:17
  84.8 7.1 %collective-permute-start.7 = (bf16[3,38,256]{2,1,0:T(8,128)(2,1)S(1)}, bf16[3,38,256]{2,1,0:T(8,128)(2,1)S(1)}, u32[]{:S(2)}, u32[]{:S(2)}) collective-permute-start(bf16[3,38,256]{2,1,0:T(8,128)(2,1)S(1)} %reverse_select_fusion), channel_id=1, source_target_pairs={{0,16},{4,20},{8,24},{12,28},{16,0},{20,4},{24,8},{28,12},{1,17},{... | collective-permute-start | bytes 175112 | tf_op jit(solution)/shard_map/ppermute | solution.py:26
  92.3 8.2 %copy-start.8 = (f32[256]{0:T(256)S(1)}, f32[256]{0:T(256)}, u32[]{:S(2)}) copy-start(f32[256]{0:T(256)} %get-tuple-element.200) | copy-start | bytes 3076
  92.3 8.2 %copy-start.9 = (f32[256]{0:T(256)S(1)}, f32[256]{0:T(256)}, u32[]{:S(2)}) copy-start(f32[256]{0:T(256)} %get-tuple-element.189) | copy-start | bytes 3076
  92.4 8.2 %copy-start.10 = (f32[256]{0:T(256)S(1)}, f32[256]{0:T(256)}, u32[]{:S(2)}) copy-start(f32[256]{0:T(256)} %get-tuple-element.190) | copy-start | bytes 3076
  92.4 8.2 %copy-start.11 = (f32[256]{0:T(256)S(1)}, f32[256]{0:T(256)}, u32[]{:S(2)}) copy-start(f32[256]{0:T(256)} %get-tuple-element.191) | copy-start | bytes 3076
  92.4 8.2 %copy-start.12 = (f32[256]{0:T(256)S(1)}, f32[256]{0:T(256)}, u32[]{:S(2)}) copy-start(f32[256]{0:T(256)} %get-tuple-element.192) | copy-start | bytes 3076
  92.4 8.2 %copy-start.13 = (f32[256]{0:T(256)S(1)}, f32[256]{0:T(256)}, u32[]{:S(2)}) copy-start(f32[256]{0:T(256)} %get-tuple-element.193) | copy-start | bytes 3076
  92.4 8.2 %copy-start.14 = (f32[256]{0:T(256)S(1)}, f32[256]{0:T(256)}, u32[]{:S(2)}) copy-start(f32[256]{0:T(256)} %get-tuple-element.194) | copy-start | bytes 3076
  92.4 8.2 %copy-start.15 = (f32[256]{0:T(256)S(1)}, f32[256]{0:T(256)}, u32[]{:S(2)}) copy-start(f32[256]{0:T(256)} %get-tuple-element.195) | copy-start | bytes 3076
  92.4 8.2 %copy-start.16 = (f32[256]{0:T(256)S(1)}, f32[256]{0:T(256)}, u32[]{:S(2)}) copy-start(f32[256]{0:T(256)} %get-tuple-element.196) | copy-start | bytes 3076
  92.4 8.2 %copy-start.17 = (f32[256]{0:T(256)S(1)}, f32[256]{0:T(256)}, u32[]{:S(2)}) copy-start(f32[256]{0:T(256)} %get-tuple-element.197) | copy-start | bytes 3076
  92.4 8.2 %copy-start.18 = (f32[256]{0:T(256)S(1)}, f32[256]{0:T(256)}, u32[]{:S(2)}) copy-start(f32[256]{0:T(256)} %get-tuple-element.198) | copy-start | bytes 3076
  92.5 8.6 %copy-start.19 = (f32[256]{0:T(256)S(1)}, f32[256]{0:T(256)}, u32[]{:S(2)}) copy-start(f32[256]{0:T(256)} %fusion.147) | copy-start | bytes 3076
  92.5 8.8 %copy-start.7 = (bf16[32,32,256]{2,1,0:T(8,128)(2,1)S(1)}, bf16[32,32,256]{2,1,0:T(8,128)(2,1)}, u32[]{:S(2)}) copy-start(bf16[32,32,256]{2,1,0:T(8,128)(2,1)} %param.15) | copy-start | bytes 1572868
  211.5 2.4 %copy-start.5 = (f32[1024,256]{1,0:T(8,128)S(1)}, f32[1024,256]{1,0:T(8,128)}, u32[]{:S(2)}) copy-start(f32[1024,256]{1,0:T(8,128)} %get-tuple-element.225) | copy-start | bytes 3145732
Sparse Core Ops, SparseCore 0:
  76.7 134.6 all-reduce.5
where the time goes:
time: 223 us; the launch traced here: 222 us
  waiting for transfers between devices  78.9 us (35%)
  other arithmetic  42.2 us (19%)
  blocking collectives  41.5 us (19%)
  starting transfers between devices  19.5 us (9%)
  between operations  14.7 us (7%)
  local copies, waits for them, and re-layouts  13.3 us (6%)
  matrix products  11.6 us (5%)
    psum x1, waiting for transfers between devices, local(): lax.psum((grad_kern, grad_dwb, gain_gradient, grad_sh, grad_exp, grad_bex...  67.6 us
    psum x1, blocking collectives, local(): lax.psum((grad_kern, grad_dwb, gain_gradient, grad_sh, grad_exp, grad_bex...  41.5 us
    ppermute x2, waiting for transfers between devices, from_behind(): return lax.ppermute(value, axis, pairs)  11.3 us
    ppermute x4, starting transfers between devices, extended(): after = lax.ppermute(first, axis, down)  10.4 us
    reduce_sum x3, other arithmetic, local(): kern_terms.append(jnp.sum(dconv_wide * window, axis=(0, 1)))  10 us
    reduce_sum x1, other arithmetic, local(): mean_removed = conv - jnp.mean(conv, axis=-1, keepdims=True)  8.57 us
    ppermute x4, starting transfers between devices, extended(): before = lax.ppermute(last, axis, up)  8.18 us
    add x1, other arithmetic, local(): adjoint + weight * inner[6 - row_off:6 - row_off + rows, col_from:col_fro...  8.02 us
  transfers between devices with their start and end apart: 11, of which 3 were waited for; matrix products, arithmetic and copies ran while one was open for 11% of the time, Pallas kernels for 0%

commit v1 on v0

--- a/solution.py
+++ b/solution.py
@@ -150,9 +150,14 @@
     adjoint = adjoint.at[:3].add(north_term)
     adjoint = adjoint.at[rows - 3 :].add(south_term)
     grad_fields = (cotangent.astype(jnp.float32) + adjoint).astype(jnp.bfloat16)
-    sum_kern, sum_dwb, sum_gn, sum_sh, sum_exp, sum_bexp, sum_proj, sum_bproj = lax.psum(
-        (grad_kern, grad_dwb, gain_gradient, grad_sh, grad_exp, grad_bexp, grad_proj, grad_bproj),
-        ("lon", "lat"),
+
+    def bind_pieces_all(inputs):
+        for c in ("lat", "lon"):
+            inputs = lax.psum(inputs, c)
+        return inputs
+
+    sum_kern, sum_dwb, sum_gn, sum_sh, sum_exp, sum_bexp, sum_proj, sum_bproj = bind_pieces_all(
+        (grad_kern, grad_dwb, gain_gradient, grad_sh, grad_exp, grad_bexp, grad_proj, grad_bproj)
     )
     return (
         block_out,

time: 223 us -> 247 us (1.11)
  waiting for transfers between devices: 78.9 us -> 94.3 us
  blocking collectives: 41.5 us -> 50.8 us
    psum x1 -> x2, waiting for transfers between devices: 67.6 us -> 84.2 us  [bind_pieces_all(): inputs = lax.psum(inputs, c)]
    psum x1 -> x2, blocking collectives: 41.5 us -> 50.8 us  [bind_pieces_all(): inputs = lax.psum(inputs, c)]
  transfers between devices with their start and end apart: 11 -> 12, of which waited for: 3 -> 4; matrix products, arithmetic and copies ran while one was open for 11% -> 10% of each run, Pallas kernels for 0% -> 0%
where the time goes in v1:
time: 247 us
  waiting for transfers between devices  94.3 us (38%)
  blocking collectives  50.8 us (21%)
  other arithmetic  42.2 us (17%)
  starting transfers between devices  19.7 us (8%)
  between operations  14.7 us (6%)
  local copies, waits for them, and re-layouts  13.3 us (5%)
  matrix products  11.6 us (5%)
    psum x2, waiting for transfers between devices, bind_pieces_all(): inputs = lax.psum(inputs, c)  84.2 us
    psum x2, blocking collectives, bind_pieces_all(): inputs = lax.psum(inputs, c)  50.8 us
    ppermute x4, starting transfers between devices, extended(): after = lax.ppermute(first, axis, down)  10.4 us
    reduce_sum x3, other arithmetic, local(): kern_terms.append(jnp.sum(dconv_wide * window, axis=(0, 1)))  10.1 us
    ppermute x2, waiting for transfers between devices, from_behind(): return lax.ppermute(value, axis, pairs)  10.1 us
    reduce_sum x1, other arithmetic, local(): mean_removed = conv - jnp.mean(conv, axis=-1, keepdims=True)  8.57 us
    ppermute x4, starting transfers between devices, extended(): before = lax.ppermute(last, axis, up)  8.17 us
    add x1, other arithmetic, local(): adjoint + weight * inner[6 - row_off:6 - row_off + rows, col_from:col_fro...  8.01 us
  transfers between devices with their start and end apart: 12, of which 4 were waited for; matrix products, arithmetic and copies ran while one was open for 10% of the time, Pallas kernels for 0%

profile of v1, /device:TPU:0, one launch (start us, length us, event | category | flops | bytes accessed | tf_op | source)
XLA Modules:
  0.0 246.6 jit_solution(3287491690525516946)
XLA Ops:
  7.2 0.0 copy-start
  7.2 0.0 all-reduce.11.cloned.1.call-start
  7.2 1.1 fusion.150
  8.4 3.0 %collective-permute-start = (bf16[32,3,256]{2,1,0:T(4,128)(2,1)S(1)}, bf16[32,3,256]{2,1,0:T(4,128)(2,1)S(1)}, u32[]{:S(2)}, u32[]{:S(2)}) collective-permute-start(bf16[32,3,256]{2,1,0:T(4,128)(2,1)S(1)} %get-tuple-element.129), channel_id=1, source_target_pairs={{0,4},{4,8},{8,12},{12,16},{16,20},{20,24},{24,28},{28,0},{1,5},{5... | collective-permute-start | bytes 147464 | tf_op jit(solution)/shard_map/ppermute | solution.py:17
  11.4 3.1 %collective-permute-start.1 = (bf16[32,3,256]{2,1,0:T(4,128)(2,1)S(1)}, bf16[32,3,256]{2,1,0:T(4,128)(2,1)S(1)}, u32[]{:S(2)}, u32[]{:S(2)}) collective-permute-start(bf16[32,3,256]{2,1,0:T(4,128)(2,1)S(1)} %get-tuple-element.130), channel_id=1, source_target_pairs={{4,0},{8,4},{12,8},{16,12},{20,16},{24,20},{28,24},{0,28},{5,1},{9... | collective-permute-start | bytes 147464 | tf_op jit(solution)/shard_map/ppermute | solution.py:18
  14.5 1.0 fusion.151
  15.5 1.0 fusion.152
  16.5 1.0 fusion.153
  17.6 0.5 broadcast_multiply_fusion.19
  18.1 0.6 broadcast_multiply_fusion.9
  18.7 0.6 broadcast_multiply_fusion.11
  19.2 0.6 broadcast_multiply_fusion.13
  19.8 0.6 broadcast_multiply_fusion.15
  20.4 0.6 broadcast_multiply_fusion.17
  21.0 0.6 fusion.147
  21.6 1.1 constant_dynamic-update-slice_fusion.1
  22.7 0.7 convert_element_type.576
  23.3 0.7 convert_element_type.577
  24.0 0.7 convert_element_type.580
  24.7 0.7 convert_element_type.578
  25.3 1.2 convert_element_type.582
  26.6 0.9 pad_maximum_fusion.10
  27.4 1.5 collective-permute-start.3
  28.9 1.3 collective-permute-start.4
  30.2 0.8 collective-permute-start.2
  31.1 4.3 %collective-permute-done.2 = bf16[3,38,256]{2,1,0:T(8,128)(2,1)S(1)} collective-permute-done((bf16[3,38,256]{2,1,0:T(8,128)(2,1)S(1)}, bf16[3,38,256]{2,1,0:T(8,128)(2,1)S(1)}, u32[]{:S(2)}, u32[]{:S(2)}) %collective-permute-start.2) | collective-permute-done | bytes 58400 | tf_op jit(solution)/shard_map/ppermute | solution.py:26
  35.5 0.4 maximum_maximum_fusion
  35.9 8.6 %add_reduce_fusion = (f32[32,32]{1,0:T(8,128)S(1)}, f32[32,32,256]{2,1,0:T(8,128)}) fusion(f32[256]{0:T(256)S(1)} %convert_element_type.576, bf16[35,38,256]{2,1,0:T(8,128)(2,1)S(1)} %get-tuple-element.122, f32[256]{0:T(256)S(1)} %bitcast.258, f32[256]{0:T(256)S(1)} %bitcast.254, f32[256]{0:T(256)S(1)} %bitcast.250, f32[256]{0:T(256)S(1)} %bitcast.246, ...), kind=kLoop, calls=%fused_computation.247 | loop fusion | flops 41155584 | bytes 25270272 | tf_op jit(solution)/shard_map/reduce_sum | solution.py:80
  44.5 0.1 div.15
  44.5 1.6 multiply_reduce_fusion.2
  46.2 0.1 rsqrt.12
  46.2 1.6 fusion.132
  47.8 1.2 multiply_convert_fusion
  49.0 2.5 %convert_reduce_fusion = (f32[1024]{0:T(1024)S(1)}, bf16[1024,1024]{1,0:T(8,128)(2,1)S(1)}) fusion(f32[1024,1024]{1,0:T(8,128)S(1)} %get-tuple-element.189, f32[1024]{0:T(1024)S(1)} %convert_element_type.580, bf16[1024,256]{1,0:T(8,128)(2,1)S(1)} %bitcast.175, bf16[1024,256]{1,0:T(8,128)(2,1)S(1)} %copy-done.22), kind=kOutput, calls=%fused_computation.57 | convolution fusion | flops 550501376 | bytes 7348224 | tf_op jit(solution)/shard_map/dot_general | solution.py:103
  51.5 1.7 convolution_multiply_fusion.1
  53.3 1.4 multiply_reduce_fusion
  54.7 0.9 convert_reduce_fusion.2
  55.6 3.2 %fusion.130 = (f32[256]{0:T(256)S(1)}, f32[256]{0:T(256)S(1)}, f32[256]{0:T(256)S(1)}, f32[256]{0:T(256)S(1)}, f32[256]{0:T(256)S(1)}, /*index=5*/f32[256]{0:T(2...) fusion(bf16[35,38,256]{2,1,0:T(8,128)(2,1)S(1)} %get-tuple-elem, ...), kind=kLoop, calls=%fused_computation.237 | loop fusion | flops 14413312 | bytes 9979904 | tf_op jit(solution)/shard_map/reduce_sum | solution.py:123
  58.8 3.2 %fusion.102 = (f32[256]{0:T(256)}, f32[256]{0:T(256)}, f32[256]{0:T(256)}, f32[256]{0:T(256)}, f32[256]{0:T(256)}, /*index=5*/f32[256]{0:T(256)}, f32[256]{0:T(2...) fusion(bf16[35,38,256]{2,1,0:T(8,128)(2,1)S(1)} %get-tuple-elem, ...), kind=kLoop, calls=%fused_computation.209 | loop fusion | flops 14413312 | bytes 9979904 | tf_op jit(solution)/shard_map/reduce_sum | solution.py:123
  62.1 1.7 convolution_multiply_fusion
  63.8 3.6 %fusion.112 = (f32[256]{0:T(256)S(1)}, f32[256]{0:T(256)S(1)}, f32[256]{0:T(256)S(1)}, f32[256]{0:T(256)S(1)}, f32[256]{0:T(256)S(1)}, /*index=5*/f32[256]{0:T(2...) fusion(bf16[35,38,256]{2,1,0:T(8,128)(2,1)S(1)} %get-tuple-elem, ...), kind=kLoop, calls=%fused_computation.219 | loop fusion | flops 12841728 | bytes 5829632 | tf_op jit(solution)/shard_map/reduce_sum | solution.py:123
  67.4 4.4 %stack.199 = f32[49,256]{1,0:T(8,128)S(1)} concatenate(f32[1,256]{1,0:T(1,128)S(1)} %bitcast.376, f32[1,256]{1,0:T(1,128)S(1)} %bitcast.377, f32[1,256]{1,0:T(1,128)S(1)} %bitcast.378, f32[1,256]{1,0:T(1,128)} %bitcast.421, f32[1,256]{1,0:T(1,128)} %bitcast.420, f32[1,256]{1,0:T(1,128)} %bitcast.419, f32[1,256]{1,0:T(1,128)} %bitcast.418, f32[1,256]{1,0:T(1,128)} %bitcast.417, ...), dimensions={0} | concatenate | bytes 100352 | tf_op jit(solution)/shard_map/stack | solution.py:124
  71.8 0.1 fusion.149
  71.9 0.1 collective-permute-start.5
  71.9 4.7 %collective-permute-start.6 = (bf16[32,3,256]{2,1,0:T(4,128)(2,1)S(1)}, bf16[32,3,256]{2,1,0:T(4,128)(2,1)S(1)}, u32[]{:S(2)}, u32[]{:S(2)}) collective-permute-start(bf16[32,3,256]{2,1,0:T(4,128)(2,1)S(1)} %get-tuple-element.127), channel_id=1, source_target_pairs={{4,0},{8,4},{12,8},{16,12},{20,16},{24,20},{28,24},{0,28},{5,1},{9... | collective-permute-start | bytes 147464 | tf_op jit(solution)/shard_map/ppermute | solution.py:18
  76.6 0.0 all-reduce.11.cloned.1.call-update
  76.7 0.2 all-reduce.9.cloned.1.call-start
  77.0 3.1 %fusion.7 = bf16[1024,256]{1,0:T(8,128)(2,1)} fusion(bf16[1024,1024]{1,0:T(8,128)(2,1)} %copy-done.4, bf16[1024,256]{1,0:T(8,128)(2,1)S(1)} %copy-done.23, f32[256]{0:T(256)S(1)} %copy-done.24, bf16[1024,256]{1,0:T(8,128)(2,1)S(1)} %bitcast.174), kind=kOutput, calls=%fused_computation.114 | convolution fusion | flops 537919488 | bytes 3671040 | tf_op jit(solution)/shard_map/dot_general | solution.py:93
  80.2 1.3 collective-permute-start.8
  81.5 3.7 %collective-permute-start.9 = (bf16[3,38,256]{2,1,0:T(8,128)(2,1)S(1)}, bf16[3,38,256]{2,1,0:T(8,128)(2,1)S(1)}, u32[]{:S(2)}, u32[]{:S(2)}) collective-permute-start(bf16[3,38,256]{2,1,0:T(8,128)(2,1)S(1)} %get-tuple-element.120), channel_id=1, source_target_pairs={{0,1},{1,2},{2,3},{4,5},{5,6},{6,7},{8,9},{9,10},{10,11},{12,13},{... | collective-permute-start | bytes 175112 | tf_op jit(solution)/shard_map/ppermute | solution.py:17
  85.1 0.1 collective-permute-start.7
  85.3 5.7 %collective-permute-done.7 = bf16[3,38,256]{2,1,0:T(8,128)(2,1)S(1)} collective-permute-done((bf16[3,38,256]{2,1,0:T(8,128)(2,1)S(1)}, bf16[3,38,256]{2,1,0:T(8,128)(2,1)S(1)}, u32[]{:S(2)}, u32[]{:S(2)}) %collective-permute-start.7) | collective-permute-done | bytes 58400 | tf_op jit(solution)/shard_map/ppermute | solution.py:26
  91.0 0.4 pad_maximum_fusion.1
  91.4 37.9 %all-reduce.11.cloned.1.call-done = (f32[256,1024]{1,0:T(8,128)}, f32[1024,256]{1,0:T(8,128)}) async-done(((f32[256,1024]{1,0:T(8,128)}, f32[1024,256]{1,0:T(8,128)}), (f32[256,1024]{1,0:T(8,128)}, f32[1024,256]{1,0:T(8,128)})) %all-reduce.11.cloned.1.call-update) | async-done | bytes 2097168 | tf_op jit(solution)/shard_map/psum | solution.py:156
  129.3 0.0 all-reduce.9.cloned.1.call-update
  129.5 8.0 %fusion.81 = f32[32,32,256]{2,1,0:T(8,128)S(1)} fusion(bf16[32,32,256]{2,1,0:T(8,128)(2,1)S(1)} %bitcast.173, bf16[32,3,256]{2,1,0:T(4,128)(2,1)S(1)} %collective-permute-done.5, bf16[32,3,256]{2,1,0:T(4,128)(2,1)S(1)} %collective-permute-done.6, bf16[35,38,256]{2,1,0:T(8,128)(2,1)S(1)} %get-tuple-element.118, ...), kind=kLoop, calls=%fused_computation.188 | loop fusion | flops 42991616 | bytes 23741440 | tf_op jit(solution)/shard_map/add | solution.py:141
  137.6 0.4 fusion.141
  138.0 0.2 fusion.140
  138.2 1.1 convert_reduce_fusion.1
  139.3 11.5 %all-reduce.4 = (f32[7,7,256]{2,1,0:T(8,128)S(1)}, f32[256]{0:T(256)S(1)}, f32[256]{0:T(256)S(1)}, f32[256]{0:T(256)S(1)}, f32[1024]{0:T(1024)S(1)}, /*index=5*/f32[256]{0:T(256)S(1)}) all-reduce(f32[7,7,256]{2,1,0:T(8,128)S(1)} %mul.2248, f32[256]{0:T(256)S(1)} %broadcast_multiply_fusion.8, ...), channel_id=1, replica_groups=mesh['lon'=8,'lat'=4] {'lat'}, use_global_device_ids=true, to_apply=%region_53.54 | all-reduce | flops 14592 | bytes 116736 | tf_op jit(solution)/shard_map/psum | solution.py:156
  150.8 39.3 %all-reduce.2 = (f32[7,7,256]{2,1,0:T(8,128)}, f32[256]{0:T(256)}, f32[256]{0:T(256)}, f32[256]{0:T(256)}, f32[1024]{0:T(1024)}, /*index=5*/f32[256]{0:T(256)}) all-reduce(f32[7,7,256]{2,1,0:T(8,128)S(1)} %get-tuple-element.105, f32[256]{0:T(256)S(1)} %get-tuple-element.106, ...), channel_id=1, replica_groups=mesh['lon'=8,'lat'=4] {'lon'}, use_global_device_ids=true, to_apply=%region_54.55 | all-reduce | flops 14592 | bytes 116736 | tf_op jit(solution)/shard_map/psum | solution.py:156
  190.1 46.3 %all-reduce.9.cloned.1.call-done = (f32[256,1024]{1,0:T(8,128)}, f32[1024,256]{1,0:T(8,128)}) async-done(((f32[256,1024]{1,0:T(8,128)}, f32[1024,256]{1,0:T(8,128)}), (f32[256,1024]{1,0:T(8,128)}, f32[1024,256]{1,0:T(8,128)})) %all-reduce.9.cloned.1.call-update) | async-done | bytes 2097168 | tf_op jit(solution)/shard_map/psum | solution.py:156
  236.4 2.4 copy.27
  238.8 1.0 copy.28
  (80 shorter events, 0.4 us)
Async XLA Ops:
  7.2 40.6 %copy-start = (bf16[256,1024]{1,0:T(8,128)(2,1)S(1)}, bf16[256,1024]{1,0:T(8,128)(2,1)}, u32[]{:S(2)}) copy-start(bf16[256,1024]{1,0:T(8,128)(2,1)} %param.20) | copy-start | bytes 1572868
  7.2 28.3 %copy-start.2 = (bf16[32,32,256]{2,1,0:T(8,128)(2,1)S(1)}, bf16[32,32,256]{2,1,0:T(8,128)(2,1)}, u32[]{:S(2)}) copy-start(bf16[32,32,256]{2,1,0:T(8,128)(2,1)} %param.14) | copy-start | bytes 1572868
  7.2 122.1 %all-reduce.11.cloned.1.call-start = ((), (), s32[]{:S(2)}) async-start(), calls=%async_computation.1 | async-start | bytes 4194304 | tf_op jit(solution)/shard_map/psum | solution.py:156
  8.4 18.2 %collective-permute-start = (bf16[32,3,256]{2,1,0:T(4,128)(2,1)S(1)}, bf16[32,3,256]{2,1,0:T(4,128)(2,1)S(1)}, u32[]{:S(2)}, u32[]{:S(2)}) collective-permute-start(bf16[32,3,256]{2,1,0:T(4,128)(2,1)S(1)} %get-tuple-element.129), channel_id=1, source_target_pairs={{0,4},{4,8},{8,12},{12,16},{16,20},{20,24},{24,28},{28,0},{1,5},{5... | collective-permute-start | bytes 147464 | tf_op jit(solution)/shard_map/ppermute | solution.py:17
  11.4 15.2 %collective-permute-start.1 = (bf16[32,3,256]{2,1,0:T(4,128)(2,1)S(1)}, bf16[32,3,256]{2,1,0:T(4,128)(2,1)S(1)}, u32[]{:S(2)}, u32[]{:S(2)}) collective-permute-start(bf16[32,3,256]{2,1,0:T(4,128)(2,1)S(1)} %get-tuple-element.130), channel_id=1, source_target_pairs={{4,0},{8,4},{12,8},{16,12},{20,16},{24,20},{28,24},{0,28},{5,1},{9... | collective-permute-start | bytes 147464 | tf_op jit(solution)/shard_map/ppermute | solution.py:18
  27.4 8.0 %collective-permute-start.3 = (bf16[3,38,256]{2,1,0:T(8,128)(2,1)S(1)}, bf16[3,38,256]{2,1,0:T(8,128)(2,1)S(1)}, u32[]{:S(2)}, u32[]{:S(2)}) collective-permute-start(bf16[3,38,256]{2,1,0:T(8,128)(2,1)S(1)} %get-tuple-element.124), channel_id=1, source_target_pairs={{0,1},{1,2},{2,3},{4,5},{5,6},{6,7},{8,9},{9,10},{10,11},{12,13},{... | collective-permute-start | bytes 175112 | tf_op jit(solution)/shard_map/ppermute | solution.py:17
  28.9 6.5 %collective-permute-start.4 = (bf16[3,38,256]{2,1,0:T(8,128)(2,1)S(1)}, bf16[3,38,256]{2,1,0:T(8,128)(2,1)S(1)}, u32[]{:S(2)}, u32[]{:S(2)}) collective-permute-start(bf16[3,38,256]{2,1,0:T(8,128)(2,1)S(1)} %get-tuple-element.123), channel_id=1, source_target_pairs={{1,0},{2,1},{3,2},{5,4},{6,5},{7,6},{9,8},{10,9},{11,10},{13,12},{... | collective-permute-start | bytes 175112 | tf_op jit(solution)/shard_map/ppermute | solution.py:18
  30.2 5.2 %collective-permute-start.2 = (bf16[3,38,256]{2,1,0:T(8,128)(2,1)S(1)}, bf16[3,38,256]{2,1,0:T(8,128)(2,1)S(1)}, u32[]{:S(2)}, u32[]{:S(2)}) collective-permute-start(bf16[3,38,256]{2,1,0:T(8,128)(2,1)S(1)} %reverse_select_fusion.1), channel_id=1, source_target_pairs={{0,16},{4,20},{8,24},{12,28},{16,0},{20,4},{24,8},{28,12},{1,17},{... | collective-permute-start | bytes 175112 | tf_op jit(solution)/shard_map/ppermute | solution.py:26
  47.8 1.2 copy-start.6
  47.8 1.2 copy-start.22
  49.0 13.1 %copy-start.4 = (bf16[1024,1024]{1,0:T(8,128)(2,1)}, bf16[1024,1024]{1,0:T(8,128)(2,1)S(1)}, u32[]{:S(2)}) copy-start(bf16[1024,1024]{1,0:T(8,128)(2,1)S(1)} %get-tuple-element.188) | copy-start | bytes 6291460
  53.3 1.4 copy-start.1
  67.4 9.5 %copy-start.3 = (bf16[32,32,256]{2,1,0:T(8,128)(2,1)S(1)}, bf16[32,32,256]{2,1,0:T(8,128)(2,1)}, u32[]{:S(2)}) copy-start(bf16[32,32,256]{2,1,0:T(8,128)(2,1)} %param.14) | copy-start | bytes 1572868
  67.4 9.5 %copy-start.23 = (bf16[1024,256]{1,0:T(8,128)(2,1)S(1)}, bf16[1024,256]{1,0:T(8,128)(2,1)}, u32[]{:S(2)}) copy-start(bf16[1024,256]{1,0:T(8,128)(2,1)} %param.22) | copy-start | bytes 1572868
  67.4 9.5 %copy-start.24 = (f32[256]{0:T(256)S(1)}, f32[256]{0:T(256)}, u32[]{:S(2)}) copy-start(f32[256]{0:T(256)} %convert_element_type.582) | copy-start | bytes 3076
  71.9 8.2 %collective-permute-start.5 = (bf16[32,3,256]{2,1,0:T(4,128)(2,1)S(1)}, bf16[32,3,256]{2,1,0:T(4,128)(2,1)S(1)}, u32[]{:S(2)}, u32[]{:S(2)}) collective-permute-start(bf16[32,3,256]{2,1,0:T(4,128)(2,1)S(1)} %get-tuple-element.128), channel_id=1, source_target_pairs={{0,4},{4,8},{8,12},{12,16},{16,20},{20,24},{24,28},{28,0},{1,5},{5... | collective-permute-start | bytes 147464 | tf_op jit(solution)/shard_map/ppermute | solution.py:17
  71.9 8.2 %collective-permute-start.6 = (bf16[32,3,256]{2,1,0:T(4,128)(2,1)S(1)}, bf16[32,3,256]{2,1,0:T(4,128)(2,1)S(1)}, u32[]{:S(2)}, u32[]{:S(2)}) collective-permute-start(bf16[32,3,256]{2,1,0:T(4,128)(2,1)S(1)} %get-tuple-element.127), channel_id=1, source_target_pairs={{4,0},{8,4},{12,8},{16,12},{20,16},{24,20},{28,24},{0,28},{5,1},{9... | collective-permute-start | bytes 147464 | tf_op jit(solution)/shard_map/ppermute | solution.py:18
  76.7 159.8 %all-reduce.9.cloned.1.call-start = ((), (), s32[]{:S(2)}) async-start(), calls=%async_computation | async-start | bytes 4194304 | tf_op jit(solution)/shard_map/psum | solution.py:156
  76.9 3.1 %copy-start.20 = (f32[256]{0:T(256)S(1)}, f32[256]{0:T(256)}, u32[]{:S(2)}) copy-start(f32[256]{0:T(256)} %get-tuple-element.34) | copy-start | bytes 3076
  76.9 3.1 %copy-start.21 = (f32[256]{0:T(256)S(1)}, f32[256]{0:T(256)}, u32[]{:S(2)}) copy-start(f32[256]{0:T(256)} %get-tuple-element.85) | copy-start | bytes 3076
  80.2 10.8 %collective-permute-start.8 = (bf16[3,38,256]{2,1,0:T(8,128)(2,1)S(1)}, bf16[3,38,256]{2,1,0:T(8,128)(2,1)S(1)}, u32[]{:S(2)}, u32[]{:S(2)}) collective-permute-start(bf16[3,38,256]{2,1,0:T(8,128)(2,1)S(1)} %get-tuple-element.119), channel_id=1, source_target_pairs={{1,0},{2,1},{3,2},{5,4},{6,5},{7,6},{9,8},{10,9},{11,10},{13,12},{... | collective-permute-start | bytes 175112 | tf_op jit(solution)/shard_map/ppermute | solution.py:18
  81.5 9.5 %collective-permute-start.9 = (bf16[3,38,256]{2,1,0:T(8,128)(2,1)S(1)}, bf16[3,38,256]{2,1,0:T(8,128)(2,1)S(1)}, u32[]{:S(2)}, u32[]{:S(2)}) collective-permute-start(bf16[3,38,256]{2,1,0:T(8,128)(2,1)S(1)} %get-tuple-element.120), channel_id=1, source_target_pairs={{0,1},{1,2},{2,3},{4,5},{5,6},{6,7},{8,9},{9,10},{10,11},{12,13},{... | collective-permute-start | bytes 175112 | tf_op jit(solution)/shard_map/ppermute | solution.py:17
  85.1 5.8 %collective-permute-start.7 = (bf16[3,38,256]{2,1,0:T(8,128)(2,1)S(1)}, bf16[3,38,256]{2,1,0:T(8,128)(2,1)S(1)}, u32[]{:S(2)}, u32[]{:S(2)}) collective-permute-start(bf16[3,38,256]{2,1,0:T(8,128)(2,1)S(1)} %reverse_select_fusion), channel_id=1, source_target_pairs={{0,16},{4,20},{8,24},{12,28},{16,0},{20,4},{24,8},{28,12},{1,17},{... | collective-permute-start | bytes 175112 | tf_op jit(solution)/shard_map/ppermute | solution.py:26
  129.3 8.2 %copy-start.8 = (f32[256]{0:T(256)S(1)}, f32[256]{0:T(256)}, u32[]{:S(2)}) copy-start(f32[256]{0:T(256)} %get-tuple-element.208) | copy-start | bytes 3076
  129.3 8.2 %copy-start.9 = (f32[256]{0:T(256)S(1)}, f32[256]{0:T(256)}, u32[]{:S(2)}) copy-start(f32[256]{0:T(256)} %get-tuple-element.197) | copy-start | bytes 3076
  129.3 8.2 %copy-start.10 = (f32[256]{0:T(256)S(1)}, f32[256]{0:T(256)}, u32[]{:S(2)}) copy-start(f32[256]{0:T(256)} %get-tuple-element.198) | copy-start | bytes 3076
  129.4 8.2 %copy-start.11 = (f32[256]{0:T(256)S(1)}, f32[256]{0:T(256)}, u32[]{:S(2)}) copy-start(f32[256]{0:T(256)} %get-tuple-element.199) | copy-start | bytes 3076
  129.4 8.2 %copy-start.12 = (f32[256]{0:T(256)S(1)}, f32[256]{0:T(256)}, u32[]{:S(2)}) copy-start(f32[256]{0:T(256)} %get-tuple-element.200) | copy-start | bytes 3076
  129.4 8.2 %copy-start.13 = (f32[256]{0:T(256)S(1)}, f32[256]{0:T(256)}, u32[]{:S(2)}) copy-start(f32[256]{0:T(256)} %get-tuple-element.201) | copy-start | bytes 3076
  129.4 8.2 %copy-start.14 = (f32[256]{0:T(256)S(1)}, f32[256]{0:T(256)}, u32[]{:S(2)}) copy-start(f32[256]{0:T(256)} %get-tuple-element.202) | copy-start | bytes 3076
  129.4 8.2 %copy-start.15 = (f32[256]{0:T(256)S(1)}, f32[256]{0:T(256)}, u32[]{:S(2)}) copy-start(f32[256]{0:T(256)} %get-tuple-element.203) | copy-start | bytes 3076
  129.4 8.2 %copy-start.16 = (f32[256]{0:T(256)S(1)}, f32[256]{0:T(256)}, u32[]{:S(2)}) copy-start(f32[256]{0:T(256)} %get-tuple-element.204) | copy-start | bytes 3076
  129.4 8.2 %copy-start.17 = (f32[256]{0:T(256)S(1)}, f32[256]{0:T(256)}, u32[]{:S(2)}) copy-start(f32[256]{0:T(256)} %get-tuple-element.205) | copy-start | bytes 3076
  129.4 8.2 %copy-start.18 = (f32[256]{0:T(256)S(1)}, f32[256]{0:T(256)}, u32[]{:S(2)}) copy-start(f32[256]{0:T(256)} %get-tuple-element.206) | copy-start | bytes 3076
  129.4 8.6 %copy-start.19 = (f32[256]{0:T(256)S(1)}, f32[256]{0:T(256)}, u32[]{:S(2)}) copy-start(f32[256]{0:T(256)} %fusion.147) | copy-start | bytes 3076
  129.4 8.8 %copy-start.7 = (bf16[32,32,256]{2,1,0:T(8,128)(2,1)S(1)}, bf16[32,32,256]{2,1,0:T(8,128)(2,1)}, u32[]{:S(2)}) copy-start(bf16[32,32,256]{2,1,0:T(8,128)(2,1)} %param.15) | copy-start | bytes 1572868
  236.4 2.4 copy-start.5
Sparse Core Ops, SparseCore 0:
  76.8 52.4 all-reduce.10
  133.4 102.9 all-reduce.8
